TPU v7x, 32 devices: a whole 2x2x4 slice. The times are simulated.
32 devices in a mesh: row: 2 (over core), col: 4 (over y, x), depth: 4 (over z).
Axes of the slice: x: 2, y: 2, z: 4, core: 2. Of those that a mesh axis runs over, the one named last changes fastest.
Arguments:
- tokens: bfloat16 [1024, 8192], P(('col', 'depth'), 'row'), may hold values from -6 to 6
- out_grad: bfloat16 [1024, 8192], P(('col', 'depth'), 'row'), may hold values from -6 to 6
- gate_w: bfloat16 [8192, 14336], P('row', ('col', 'depth')), may hold values from -0.09375 to 0.09375
- up_w: bfloat16 [8192, 14336], P('row', ('col', 'depth')), may hold values from -0.09375 to 0.09375
- down_w: bfloat16 [14336, 8192], P(('col', 'depth'), 'row'), may hold values from -0.0625 to 0.0625
- keep_gate: int32 [64, 112], P('row', ('col', 'depth')), may hold values from 0 to 1, as said below
- keep_up: int32 [64, 112], P('row', ('col', 'depth')), may hold values from 0 to 1, as said below
- keep_down: int32 [112, 64], P(('col', 'depth'), 'row'), may hold values from 0 to 1, as said below
- exp_gate: int32 [64, 112], P('row', ('col', 'depth')), may hold values from -1 to 1
- exp_up: int32 [64, 112], P('row', ('col', 'depth')), may hold values from -1 to 1
- exp_down: int32 [112, 64], P(('col', 'depth'), 'row'), may hold values from -1 to 1
Outputs:
- output: bfloat16 [1024, 8192], P(('col', 'depth'), 'row')
- input_grad: bfloat16 [1024, 8192], P(('col', 'depth'), 'row')
- gate_w_grad: bfloat16 [8192, 14336], P('row', ('col', 'depth'))
- up_w_grad: bfloat16 [8192, 14336], P('row', ('col', 'depth'))
- down_w_grad: bfloat16 [14336, 8192], P(('col', 'depth'), 'row')
Inputs may be any that keep to these rules, and one draw needn't show every extreme that they name: `keep_gate`: 1 where a weight block is kept, 0 where it is dropped; the share kept may differ from one block column to another. `keep_up`: 1 where a weight block is kept, 0 where it is dropped; the share kept may differ from one block column to another. `keep_down`: 1 where a weight block is kept, 0 where it is dropped; the share kept may differ from one block column to another.
All inputs are finite; a program needn't handle non-finite values.
Results may differ from a plain program's by a relative error of at most 0.005.
Values may be sent and summed in bfloat16 or wider, within the bound.
A program may use at most 256 MiB of HBM per device.

v0:
```python
import jax
import jax.numpy as jnp
from jax import lax
from jax.sharding import PartitionSpec as P


def block_factor(keep, exps):
    return keep.astype(jnp.float32) * jnp.exp2(exps.astype(jnp.float32))


def scaled(raw, factor):
    rows, cols = factor.shape
    high = raw.shape[0] // rows
    wide = raw.shape[1] // cols
    blocks = raw.reshape(rows, high, cols, wide) * factor.astype(jnp.bfloat16)[:, None, :, None]
    return blocks.reshape(raw.shape)


def masked_grad(grad, factor):
    rows, cols = factor.shape
    blocks = (
        grad.reshape(rows, grad.shape[0] // rows, cols, grad.shape[1] // cols)
        * factor[:, None, :, None]
    )
    return blocks.reshape(grad.shape).astype(jnp.bfloat16)


def activate(gate, up, hidden_grad):
    sig = jax.nn.sigmoid(gate)
    hidden = (gate * sig * up).astype(jnp.bfloat16)
    gate_grad = (hidden_grad * up * sig * (1.0 + gate * (1.0 - sig))).astype(jnp.bfloat16)
    up_grad = (hidden_grad * gate * sig).astype(jnp.bfloat16)
    return (hidden, gate_grad, up_grad)


def shards(
    tokens,
    out_grad,
    gate_w,
    up_w,
    down_w,
    keep_gate,
    keep_up,
    keep_down,
    exp_gate,
    exp_up,
    exp_down,
):
    factor_gate = block_factor(keep_gate, exp_gate)
    factor_up = block_factor(keep_up, exp_up)
    factor_down = block_factor(keep_down, exp_down)
    eff_gate = scaled(gate_w, factor_gate)
    eff_up = scaled(up_w, factor_up)
    eff_down = scaled(down_w, factor_down)
    panel = gate_w.shape[0]
    width = gate_w.shape[1]
    paired = jnp.concatenate([eff_gate, eff_up], axis=1)
    gathered_in, gathered_grad = (
        lax.all_gather(tokens, ("col", "depth"), axis=0, tiled=True),
        lax.all_gather(out_grad, ("col", "depth"), axis=0, tiled=True),
    )
    sums = lax.psum_scatter(
        jnp.concatenate(
            [
                jnp.dot(gathered_in, paired, preferred_element_type=jnp.float32),
                jnp.dot(gathered_grad, eff_down.T, preferred_element_type=jnp.float32),
            ],
            axis=1,
        ),
        "row",
        scatter_dimension=0,
        tiled=True,
    )
    hidden, gate_grad, up_grad = activate(
        sums[:, :width], sums[:, width : 2 * width], sums[:, 2 * width :]
    )
    whole = lax.all_gather(
        jnp.concatenate([hidden, gate_grad, up_grad], axis=1), "row", axis=0, tiled=True
    )
    hidden_all = whole[:, :width]
    pair_grad = whole[:, width:]
    result = lax.psum_scatter(
        jnp.concatenate(
            [
                jnp.dot(hidden_all, eff_down, preferred_element_type=jnp.float32),
                jnp.dot(pair_grad, paired.T, preferred_element_type=jnp.float32),
            ],
            axis=1,
        ),
        ("col", "depth"),
        scatter_dimension=0,
        tiled=True,
    )
    output = result[:, :panel].astype(jnp.bfloat16)
    input_grad = result[:, panel:].astype(jnp.bfloat16)
    pair_weights = jnp.dot(gathered_in.T, pair_grad, preferred_element_type=jnp.float32)
    gate_w_grad = masked_grad(pair_weights[:, :width], factor_gate)
    up_w_grad = masked_grad(pair_weights[:, width:], factor_up)
    down_w_grad = masked_grad(
        jnp.dot(hidden_all.T, gathered_grad, preferred_element_type=jnp.float32), factor_down
    )
    return (output, input_grad, gate_w_grad, up_w_grad, down_w_grad)


def solution(mesh):
    return jax.shard_map(
        shards,
        mesh=mesh,
        in_specs=(
            P(("col", "depth"), "row"),
            P(("col", "depth"), "row"),
            P("row", ("col", "depth")),
            P("row", ("col", "depth")),
            P(("col", "depth"), "row"),
            P("row", ("col", "depth")),
            P("row", ("col", "depth")),
            P(("col", "depth"), "row"),
            P("row", ("col", "depth")),
            P("row", ("col", "depth")),
            P(("col", "depth"), "row"),
        ),
        out_specs=(
            P(("col", "depth"), "row"),
            P(("col", "depth"), "row"),
            P("row", ("col", "depth")),
            P("row", ("col", "depth")),
            P(("col", "depth"), "row"),
        ),
        check_vma=False,
    )
```

profile of v0, /device:TPU:0, one launch (start us, length us, event | category | flops | bytes accessed | tf_op | source)
XLA Modules:
  0.0 1067.9 jit_solution(7671832824906796205)
XLA Ops:
  7.2 0.0 all-gather.6.cloned.1.call-start
  7.2 0.7 all-gather.6.cloned.1.call-update
  7.9 0.0 all-gather.4.cloned.1.call-start
  7.9 0.7 all-gather.4.cloned.1.call-update
  8.6 0.0 reduce-scatter.3.cloned.1.call-start
  8.7 10.8 %copy.20 = bf16[4096,896]{0,1:T(8,128)(2,1)} copy(bf16[4096,896]{1,0:T(8,128)(2,1)} %param.13) | data formatting | bytes 14680064 | tf_op args[2]
  19.5 0.0 copy-start.9
  19.5 0.0 copy-start.10
  19.5 11.1 %copy.21 = bf16[4096,896]{0,1:T(8,128)(2,1)} copy(bf16[4096,896]{1,0:T(8,128)(2,1)} %param.14) | data formatting | bytes 14680064 | tf_op args[3]
  30.6 0.0 copy-done.6
  30.6 0.6 fusion.14
  31.2 0.6 fusion.15
  31.8 0.6 fusion.13
  32.4 1.0 mul.104
  33.5 4.7 mul.100
  38.2 1.7 copy-done
  39.9 10.6 bitcast_multiply_fusion.4
  50.5 75.3 %all-gather.6.cloned.1.call-done = bf16[1024,4096]{1,0:T(8,128)(2,1)} async-done(((bf16[64,4096]{1,0:T(8,128)(2,1)}), bf16[1024,4096]{1,0:T(8,128)(2,1)}) %all-gather.6.cloned.1.call-update) | async-done | bytes 8388624 | tf_op jit(solution)/shard_map/all_gather | solution.py:60
  125.8 1.0 mul.108
  126.9 2.9 copy-done.1
  129.8 16.3 %convolution_bitcast_fusion.1 = f32[1024,896]{0,1:T(8,128)} fusion(bf16[1024,4096]{1,0:T(8,128)(2,1)} %all-gather.6.cloned.1.call-done, bf16[896,4096]{1,0:T(8,128)(2,1)} %param.15, bf16[112,8,32,128]{3,2,1,0:T(8,128)(2,1)S(1)} %bitcast.54), kind=kOutput, calls=%fused_computation.19 | convolution fusion | flops 7519862784 | bytes 26738688 | tf_op jit(solution)/shard_map/dot_general | solution.py:66
  146.0 93.1 %all-gather.4.cloned.1.call-done = bf16[1024,4096]{1,0:T(8,128)(2,1)} async-done(((bf16[64,4096]{1,0:T(8,128)(2,1)}), bf16[1024,4096]{1,0:T(8,128)(2,1)}) %all-gather.4.cloned.1.call-update) | async-done | bytes 8388624 | tf_op jit(solution)/shard_map/all_gather | solution.py:59
  239.1 22.9 %fusion.5 = f32[1024,1792]{0,1:T(8,128)} fusion(bf16[1024,4096]{1,0:T(8,128)(2,1)} %all-gather.4.cloned.1.call-done, bf16[4096,896]{0,1:T(8,128)(2,1)} %get-tuple-element.28, bf16[4096,896]{0,1:T(8,128)(2,1)} %get-tuple-element.29), kind=kOutput, calls=%fused_computation.15 | convolution fusion | flops 15061745664 | bytes 30408704 | tf_op jit(solution)/shard_map/dot_general | solution.py:65
  262.0 10.7 %pad_maximum_fusion.2 = f32[1024,2688]{0,1:T(8,128)} fusion(f32[1024,896]{0,1:T(8,128)} %convolution_bitcast_fusion.1, f32[1024,1792]{0,1:T(8,128)} %fusion.5), kind=kLoop, calls=%fused_computation.9 | loop fusion | flops 2752512 | bytes 22020096 | tf_op jit(solution)/shard_map/concatenate | solution.py:63
  272.7 0.0 reduce-scatter.3.cloned.1.call-update
  272.8 0.0 all-gather.8.cloned.1.call-start
  272.8 16.5 %reduce-scatter.3.cloned.1.call-done = f32[512,2688]{0,1:T(8,128)} async-done(((f32[1024,2688]{0,1:T(8,128)}), f32[512,2688]{0,1:T(8,128)}) %reduce-scatter.3.cloned.1.call-update) | async-done | bytes 5505040 | tf_op jit(solution)/shard_map/reduce_scatter | solution.py:62
  289.3 3.7 multiply_convert_fusion.2
  293.0 1.7 pad_maximum_fusion.7
  294.8 0.0 all-gather.8.cloned.1.call-update
  294.8 0.0 reduce-scatter.5.cloned.1.call-start
  294.8 17.0 %all-gather.8.cloned.1.call-done = bf16[1024,2688]{0,1:T(8,128)(2,1)} async-done(((bf16[512,2688]{0,1:T(8,128)(2,1)}), bf16[1024,2688]{0,1:T(8,128)(2,1)}) %all-gather.8.cloned.1.call-update) | async-done | bytes 5505040 | tf_op jit(solution)/shard_map/all_gather | solution.py:77
  311.8 23.3 %fusion.3 = f32[1024,4096]{1,0:T(8,128)} fusion(bf16[4096,896]{0,1:T(8,128)(2,1)} %get-tuple-element.28, bf16[4096,896]{0,1:T(8,128)(2,1)} %get-tuple-element.29, bf16[1024,2688]{0,1:T(8,128)(2,1)} %all-gather.8.cloned.1.call-done), kind=kOutput, calls=%fused_computation.10 | convolution fusion | flops 15061745664 | bytes 35127296 | tf_op jit(solution)/shard_map/dot_general | solution.py:86
  335.2 13.4 %fusion.8 = f32[1024,4096]{1,0:T(8,128)S(1)} fusion(bf16[896,4096]{1,0:T(8,128)(2,1)} %param.15, bf16[112,8,32,128]{3,2,1,0:T(8,128)(2,1)} %bitcast.55, bf16[1024,2688]{0,1:T(8,128)(2,1)} %all-gather.8.cloned.1.call-done), kind=kOutput, calls=%fused_computation.20 | convolution fusion | flops 7519862784 | bytes 33292288 | tf_op jit(solution)/shard_map/dot_general | solution.py:85
  348.6 18.3 %pad_maximum_fusion = f32[1024,8192]{1,0:T(8,128)} fusion(f32[1024,4096]{1,0:T(8,128)} %fusion.3, f32[1024,4096]{1,0:T(8,128)S(1)} %fusion.8), kind=kLoop, calls=%fused_computation | loop fusion | flops 8388608 | bytes 67108864 | tf_op jit(solution)/shard_map/concatenate | solution.py:83
  367.0 0.0 reduce-scatter.5.cloned.1.call-update
  367.0 0.0 copy-start.4
  367.0 23.2 %convolution_bitcast_fusion = f32[4096,1792]{0,1:T(8,128)} fusion(bf16[1024,4096]{1,0:T(8,128)(2,1)} %all-gather.4.cloned.1.call-done, bf16[1024,2688]{0,1:T(8,128)(2,1)} %all-gather.8.cloned.1.call-done), kind=kOutput, calls=%fused_computation.1 | convolution fusion | flops 15032385536 | bytes 41418752 | tf_op jit(solution)/shard_map/dot_general | solution.py:96
  390.2 1.9 mul.122
  392.1 7.1 mul.119
  399.3 26.2 %fusion.1 = (bf16[4096,896]{0,1:T(8,128)(2,1)}, bf16[4096,896]{0,1:T(8,128)(2,1)}) fusion(f32[112,8,32,128]{3,2,1,0:T(8,128)S(1)} %bitcast.50, f32[4096,1792]{0,1:T(8,128)} %convolution_bitcast_fusion, f32[112,8,32,128]{3,2,1,0:T(8,128)} %bitcast.51), kind=kLoop, calls=%fused_computation.5 | loop fusion | flops 14680064 | bytes 73400320 | tf_op jit(solution)/shard_map/convert_element_type | solution.py:25
  425.5 10.9 %copy.23 = bf16[4096,896]{1,0:T(8,128)(2,1)} copy(bf16[4096,896]{0,1:T(8,128)(2,1)} %get-tuple-element.21) | data formatting | bytes 14680064
  436.4 10.8 %copy.22 = bf16[4096,896]{1,0:T(8,128)(2,1)} copy(bf16[4096,896]{0,1:T(8,128)(2,1)} %get-tuple-element.22) | data formatting | bytes 14680064
  447.2 7.1 mul.125
  454.3 24.6 %fusion = bf16[896,4096]{1,0:T(8,128)(2,1)} fusion(f32[112,8,32,128]{3,2,1,0:T(8,128)} %bitcast.58, bf16[1024,4096]{1,0:T(8,128)(2,1)} %all-gather.6.cloned.1.call-done, bf16[1024,2688]{0,1:T(8,128)(2,1)} %all-gather.8.cloned.1.call-done), kind=kOutput, calls=%fused_computation.3 | convolution fusion | flops 7523532800 | bytes 32243712 | tf_op jit(solution)/shard_map/dot_general | solution.py:100
  478.9 579.2 %reduce-scatter.5.cloned.1.call-done = f32[64,8192]{1,0:T(8,128)} async-done(((f32[1024,8192]{1,0:T(8,128)}), f32[64,8192]{1,0:T(8,128)}) %reduce-scatter.5.cloned.1.call-update) | async-done | bytes 2097168 | tf_op jit(solution)/shard_map/reduce_scatter | solution.py:82
  1058.2 1.7 convert.4
  1059.9 1.0 fusion.16
  (21 shorter events, 0.0 us)
Async XLA Ops:
  7.2 118.7 %all-gather.6.cloned.1.call-start = ((), (), s32[]{:S(2)}) async-start(), calls=%async_computation.3 | async-start | bytes 8912896 | tf_op jit(solution)/shard_map/all_gather | solution.py:60
  7.9 231.2 %all-gather.4.cloned.1.call-start = ((), (), s32[]{:S(2)}) async-start(), calls=%async_computation.2 | async-start | bytes 8912896 | tf_op jit(solution)/shard_map/all_gather | solution.py:59
  8.6 280.7 %reduce-scatter.3.cloned.1.call-start = ((), (), s32[]{:S(2)}) async-start(), calls=%async_computation.4 | async-start | bytes 16515072 | tf_op jit(solution)/shard_map/reduce_scatter | solution.py:62
  19.5 11.1 %copy-start.5 = (s32[32,7]{0,1:T(8,128)S(1)}, s32[32,7]{0,1:T(8,128)}, u32[]{:S(2)}) copy-start(s32[32,7]{0,1:T(8,128)} %param.19) | copy-start | bytes 2692
  19.5 11.1 %copy-start.6 = (s32[32,7]{0,1:T(8,128)S(1)}, s32[32,7]{0,1:T(8,128)}, u32[]{:S(2)}) copy-start(s32[32,7]{0,1:T(8,128)} %param.16) | copy-start | bytes 2692
  19.5 11.7 %copy-start.7 = (s32[32,7]{0,1:T(8,128)S(1)}, s32[32,7]{0,1:T(8,128)}, u32[]{:S(2)}) copy-start(s32[32,7]{0,1:T(8,128)} %param.20) | copy-start | bytes 2692
  19.5 11.7 %copy-start.8 = (s32[32,7]{0,1:T(8,128)S(1)}, s32[32,7]{0,1:T(8,128)}, u32[]{:S(2)}) copy-start(s32[32,7]{0,1:T(8,128)} %param.17) | copy-start | bytes 2692
  19.5 12.3 %copy-start.9 = (s32[7,32]{1,0:T(8,128)S(1)}, s32[7,32]{1,0:T(8,128)}, u32[]{:S(2)}) copy-start(s32[7,32]{1,0:T(8,128)} %param.21) | copy-start | bytes 2692
  19.5 12.3 %copy-start.10 = (s32[7,32]{1,0:T(8,128)S(1)}, s32[7,32]{1,0:T(8,128)}, u32[]{:S(2)}) copy-start(s32[7,32]{1,0:T(8,128)} %param.18) | copy-start | bytes 2692
  31.8 6.4 slice-start
  32.4 5.8 slice-start.1
  32.4 7.5 copy-start
  126.9 2.9 copy-start.1
  272.8 39.1 %all-gather.8.cloned.1.call-start = ((), (), s32[]{:S(2)}) async-start(), calls=%async_computation.5 | async-start | bytes 8257536 | tf_op jit(solution)/shard_map/all_gather | solution.py:77
  294.8 763.4 %reduce-scatter.5.cloned.1.call-start = ((), (), s32[]{:S(2)}) async-start(), calls=%async_computation.6 | async-start | bytes 35651584 | tf_op jit(solution)/shard_map/reduce_scatter | solution.py:82
  367.0 23.2 %copy-start.4 = (f32[32,7]{0,1:T(8,128)S(1)}, f32[32,7]{0,1:T(8,128)}, u32[]{:S(2)}) copy-start(f32[32,7]{0,1:T(8,128)} %get-tuple-element.20) | copy-start | bytes 2692
  390.2 1.9 copy-start.3
  436.4 10.8 %copy-start.2 = (f32[7,32]{1,0:T(8,128)S(1)}, f32[7,32]{1,0:T(8,128)}, u32[]{:S(2)}) copy-start(f32[7,32]{1,0:T(8,128)} %get-tuple-element.16) | copy-start | bytes 2692
Sparse Core Ops, SparseCore 0:
  10.8 115.0 all-gather.5
  128.6 110.4 all-gather.3
  272.9 16.3 reduce-scatter.2
  294.9 16.8 all-gather.7
  367.1 691.0 reduce-scatter.4
where the time goes:
time: 1080 us; the launch traced here: 1070 us
  waiting for transfers between devices  783 us (72%)
  matrix products  124 us (11%)
  other arithmetic  74.9 us (7%)
  local copies, waits for them, and re-layouts  72.2 us (7%)
  between operations  14.4 us (1%)
    reduce_scatter x1, waiting for transfers between devices, shards(): lax.psum_scatter(jnp.concatenate([jnp.dot(hidden_all, eff_down, preferred...  579 us
    all_gather x1, waiting for transfers between devices, shards(): lax.all_gather(tokens, ('col', 'depth'), axis=0, tiled=True)  93.1 us
    all_gather x1, waiting for transfers between devices, shards(): lax.all_gather(out_grad, ('col', 'depth'), axis=0, tiled=True)  75.3 us
    unnamed x30, local copies, waits for them, and re-layouts  48.2 us
    convert_element_type x1, other arithmetic, masked_grad(): return blocks.reshape(grad.shape).astype(jnp.bfloat16)  26.2 us
    dot_general x1, matrix products, shards(): jnp.dot(hidden_all.T, gathered_grad, preferred_element_type=jnp.float32)  24.6 us
    dot_general x1, matrix products, shards(): jnp.dot(pair_grad, paired.T, preferred_element_type=jnp.float32)  23.3 us
    dot_general x1, matrix products, shards(): jnp.dot(gathered_in.T, pair_grad, preferred_element_type=jnp.float32)  23.2 us
  transfers between devices with their start and end apart: 5, of which 5 were waited for; matrix products, arithmetic and copies ran while one was open for 16% of the time, Pallas kernels for 0%

commit v1 on v0

--- a/solution.py
+++ b/solution.py
@@ -2,6 +2,18 @@
 import jax.numpy as jnp
 from jax import lax
 from jax.sharding import PartitionSpec as P
+
+
+def doubled_up(value, axis, dim):
+    ways, here = (lax.axis_size(axis), lax.axis_index(axis))
+    grown, reach = (value, 1)
+    while reach < ways:
+        theirs = lax.ppermute(grown, axis, [(d, d ^ reach) for d in range(ways)])
+        mine_first = jnp.concatenate([grown, theirs], axis=dim)
+        theirs_first = jnp.concatenate([theirs, grown], axis=dim)
+        grown = jnp.where(here & reach == 0, mine_first, theirs_first)
+        reach = 2 * reach
+    return grown
 
 
 def block_factor(keep, exps):
@@ -56,7 +68,7 @@
     width = gate_w.shape[1]
     paired = jnp.concatenate([eff_gate, eff_up], axis=1)
     gathered_in, gathered_grad = (
-        lax.all_gather(tokens, ("col", "depth"), axis=0, tiled=True),
+        doubled_up(tokens, ("col", "depth"), 0),
         lax.all_gather(out_grad, ("col", "depth"), axis=0, tiled=True),
     )
     sums = lax.psum_scatter(

time: 1080 us -> 1140 us (1.056)
  local copies, waits for them, and re-layouts: 72.2 us -> 139 us
  waiting for transfers between devices: 783 us -> 766 us
    ppermute x0 -> x4, waiting for transfers between devices: none -> 213 us  [doubled_up(): theirs = lax.ppermute(grown, axis, [(d, d ^ reach) for d in range(ways)])]
    all_gather x1 -> x0, waiting for transfers between devices: 93.1 us -> none  [shards(): lax.all_gather(tokens, ('col', 'depth'), axis=0, tiled=True)]
    all_gather x1, waiting for transfers between devices: 75.3 us -> 0.01 us  [shards(): lax.all_gather(out_grad, ('col', 'depth'), axis=0, tiled=True)]
    reduce_scatter x1, waiting for transfers between devices: 579 us -> 517 us  [shards(): lax.psum_scatter(jnp.concatenate([jnp.dot(hidden_all, eff_down, preferred...]
    mul x3 -> x5, local copies, waits for them, and re-layouts: 16.2 us -> 54.1 us  [masked_grad(): grad.reshape(rows, grad.shape[0] // rows, cols, grad.shape[1] // cols)]
    unnamed x30 -> x36, local copies, waits for them, and re-layouts: 48.2 us -> 77.2 us
  transfers between devices with their start and end apart: 5 -> 8, of which waited for: 5 -> 7; matrix products, arithmetic and copies ran while one was open for 16% -> 22% of each run, Pallas kernels for 0% -> 0%
where the time goes in v1:
time: 1140 us; the launch traced here: 1130 us
  waiting for transfers between devices  766 us (67%)
  local copies, waits for them, and re-layouts  139 us (12%)
  matrix products  125 us (11%)
  other arithmetic  80.3 us (7%)
  between operations  14.3 us (1%)
    reduce_scatter x1, waiting for transfers between devices, shards(): lax.psum_scatter(jnp.concatenate([jnp.dot(hidden_all, eff_down, preferred...  517 us
    ppermute x4, waiting for transfers between devices, doubled_up(): theirs = lax.ppermute(grown, axis, [(d, d ^ reach) for d in range(ways)])  213 us
    unnamed x36, local copies, waits for them, and re-layouts  77.2 us
    mul x5, local copies, waits for them, and re-layouts, masked_grad(): grad.reshape(rows, grad.shape[0] // rows, cols, grad.shape[1] // cols)  54.1 us
    convert_element_type x1, other arithmetic, masked_grad(): return blocks.reshape(grad.shape).astype(jnp.bfloat16)  24.7 us
    dot_general x1, matrix products, shards(): jnp.dot(gathered_in.T, pair_grad, preferred_element_type=jnp.float32)  23.8 us
    dot_general x1, matrix products, shards(): jnp.dot(pair_grad, paired.T, preferred_element_type=jnp.float32)  23.1 us
  transfers between devices with their start and end apart: 8, of which 7 were waited for; matrix products, arithmetic and copies ran while one was open for 22% of the time, Pallas kernels for 0%

profile of v1, /device:TPU:0, one launch (start us, length us, event | category | flops | bytes accessed | tf_op | source)
XLA Modules:
  0.0 1133.7 jit_solution(312314134784099285)
XLA Ops:
  7.2 0.7 all-gather.3.cloned.1.call-update
  7.9 3.1 collective-permute-start
  11.1 12.1 %collective-permute-done = bf16[64,4096]{1,0:T(8,128)(2,1)S(1)} collective-permute-done((bf16[64,4096]{1,0:T(8,128)(2,1)}, bf16[64,4096]{1,0:T(8,128)(2,1)S(1)}, u32[]{:S(2)}, u32[]{:S(2)}) %collective-permute-start) | collective-permute-done | bytes 524320 | tf_op jit(solution)/shard_map/ppermute | solution.py:11
  23.2 1.4 maximum_select_fusion.5
  24.6 2.8 collective-permute-start.1
  27.5 76.9 %collective-permute-done.1 = bf16[128,4096]{1,0:T(8,128)(2,1)} collective-permute-done((bf16[128,4096]{1,0:T(8,128)(2,1)S(1)}, bf16[128,4096]{1,0:T(8,128)(2,1)}, u32[]{:S(2)}, u32[]{:S(2)}) %collective-permute-start.1) | collective-permute-done | bytes 1048608 | tf_op jit(solution)/shard_map/ppermute | solution.py:11
  104.4 2.3 maximum_select_fusion.2
  106.7 1.6 collective-permute-start.2
  108.3 75.6 %collective-permute-done.2 = bf16[256,4096]{1,0:T(8,128)(2,1)} collective-permute-done((bf16[256,4096]{1,0:T(8,128)(2,1)S(1)}, bf16[256,4096]{1,0:T(8,128)(2,1)}, u32[]{:S(2)}, u32[]{:S(2)}) %collective-permute-start.2) | collective-permute-done | bytes 2097184 | tf_op jit(solution)/shard_map/ppermute | solution.py:11
  183.9 4.6 maximum_select_fusion.1
  188.5 1.4 collective-permute-start.3
  189.9 10.8 copy.21
  200.7 10.8 copy.22
  211.5 0.6 fusion.15
  212.1 0.6 fusion.16
  212.7 0.6 fusion.14
  213.4 1.0 mul.108
  214.4 4.7 mul.104
  219.1 1.7 copy-done
  220.8 10.6 bitcast_multiply_fusion.2
  231.4 48.5 %collective-permute-done.3 = bf16[512,4096]{1,0:T(8,128)(2,1)} collective-permute-done((bf16[512,4096]{1,0:T(8,128)(2,1)}, bf16[512,4096]{1,0:T(8,128)(2,1)}, u32[]{:S(2)}, u32[]{:S(2)}) %collective-permute-start.3) | collective-permute-done | bytes 4194336 | tf_op jit(solution)/shard_map/ppermute | solution.py:11
  279.9 22.6 %fusion.4 = f32[1024,1792]{1,0:T(8,128)} fusion(bf16[4096,896]{0,1:T(8,128)(2,1)} %get-tuple-element.18, bf16[4096,896]{0,1:T(8,128)(2,1)} %get-tuple-element.19, bf16[512,4096]{1,0:T(8,128)(2,1)} %collective-permute-done.3, bf16[512,4096]{1,0:T(8,128)(2,1)} %maximum_select_fusion.1, pred[]{:T(512)S(6)} %eq.12), kind=kOutput, calls=%fused_computation.12 | convolution fusion | flops 15099494400 | bytes 30408704 | tf_op jit(solution)/shard_map/dot_general | solution.py:77
  302.6 1.0 mul.112
  303.6 2.9 copy-done.2
  306.5 18.7 %convolution_bitcast_fusion = f32[1024,896]{1,0:T(8,128)} fusion(bf16[1024,4096]{1,0:T(8,128)(2,1)} %all-gather.3.cloned.1.call-done, bf16[896,4096]{1,0:T(8,128)(2,1)} %param.15, bf16[112,8,32,128]{3,2,1,0:T(8,128)(2,1)S(1)} %bitcast.51), kind=kOutput, calls=%fused_computation.23 | convolution fusion | flops 7519862784 | bytes 26738688 | tf_op jit(solution)/shard_map/dot_general | solution.py:78
  325.2 9.1 pad_maximum_fusion.2
  334.3 0.0 all-gather.5.cloned.1.call-start
  334.4 17.8 %reduce-scatter.3.cloned.1.call-done = f32[512,2688]{1,0:T(8,128)} async-done(((f32[1024,2688]{1,0:T(8,128)}), f32[512,2688]{1,0:T(8,128)}) %reduce-scatter.3.cloned.1.call-update) | async-done | bytes 5505040 | tf_op jit(solution)/shard_map/reduce_scatter | solution.py:74
  352.2 3.6 multiply_convert_fusion.2
  355.8 1.7 pad_maximum_fusion.5
  357.6 17.0 %all-gather.5.cloned.1.call-done = bf16[1024,2688]{1,0:T(8,128)(2,1)} async-done(((bf16[512,2688]{1,0:T(8,128)(2,1)}), bf16[1024,2688]{1,0:T(8,128)(2,1)}) %all-gather.5.cloned.1.call-update) | async-done | bytes 5505040 | tf_op jit(solution)/shard_map/all_gather | solution.py:89
  374.6 23.1 %fusion.3 = f32[1024,4096]{1,0:T(8,128)} fusion(bf16[4096,896]{0,1:T(8,128)(2,1)} %get-tuple-element.18, bf16[4096,896]{0,1:T(8,128)(2,1)} %get-tuple-element.19, bf16[1024,2688]{1,0:T(8,128)(2,1)} %all-gather.5.cloned.1.call-done), kind=kOutput, calls=%fused_computation.11 | convolution fusion | flops 15061745664 | bytes 35127296 | tf_op jit(solution)/shard_map/dot_general | solution.py:98
  397.7 16.2 %fusion.8 = f32[1024,4096]{1,0:T(8,128)} fusion(bf16[896,4096]{1,0:T(8,128)(2,1)} %param.15, bf16[112,8,32,128]{3,2,1,0:T(8,128)(2,1)} %bitcast.52, bf16[1024,2688]{1,0:T(8,128)(2,1)} %all-gather.5.cloned.1.call-done), kind=kOutput, calls=%fused_computation.24 | convolution fusion | flops 7519862784 | bytes 33292288 | tf_op jit(solution)/shard_map/dot_general | solution.py:97
  413.9 18.8 %pad_maximum_fusion = f32[1024,8192]{1,0:T(8,128)} fusion(f32[1024,4096]{1,0:T(8,128)S(1)} %copy-done.1, f32[1024,4096]{1,0:T(8,128)} %fusion.8), kind=kLoop, calls=%fused_computation | loop fusion | flops 8388608 | bytes 67108864 | tf_op jit(solution)/shard_map/concatenate | solution.py:95
  432.8 0.7 copy-done.5
  433.4 7.6 mul.126
  441.0 25.1 %copy.41 = f32[112,8,32,128]{3,1,2,0:T(8,128)} copy(f32[112,8,32,128]{3,2,1,0:T(8,128)} %bitcast.44) | data formatting | bytes 29360128
  466.1 16.2 %copy.25 = f32[4096,896]{1,0:T(8,128)} copy(f32[4096,896]{0,1:T(8,128)} %bitcast.42) | data formatting | bytes 29360128 | tf_op jit(solution)/shard_map/mul | solution.py:34
  482.3 7.0 mul.123
  489.3 25.2 %copy.42 = f32[112,8,32,128]{3,1,2,0:T(8,128)} copy(f32[112,8,32,128]{3,2,1,0:T(8,128)} %bitcast.45) | data formatting | bytes 29360128
  514.5 16.2 %copy.24 = f32[4096,896]{1,0:T(8,128)} copy(f32[4096,896]{0,1:T(8,128)} %bitcast.43) | data formatting | bytes 29360128 | tf_op jit(solution)/shard_map/mul | solution.py:34
  530.7 7.1 mul.129
  537.8 20.7 %fusion = bf16[896,4096]{1,0:T(8,128)(2,1)} fusion(f32[112,8,32,128]{3,2,1,0:T(8,128)} %bitcast.46, bf16[1024,4096]{1,0:T(8,128)(2,1)} %all-gather.3.cloned.1.call-done, bf16[1024,2688]{1,0:T(8,128)(2,1)} %all-gather.5.cloned.1.call-done), kind=kOutput, calls=%fused_computation.2 | convolution fusion | flops 7523532800 | bytes 32243712 | tf_op jit(solution)/shard_map/dot_general | solution.py:112
  558.6 23.8 %fusion.5 = f32[4096,1792]{1,0:T(8,128)} fusion(bf16[1024,2688]{1,0:T(8,128)(2,1)S(1)} %bitcast.54, bf16[512,4096]{1,0:T(8,128)(2,1)} %collective-permute-done.3, bf16[512,4096]{1,0:T(8,128)(2,1)} %maximum_select_fusion.1, pred[]{:T(512)S(6)} %eq.12), kind=kOutput, calls=%fused_computation.18 | convolution fusion | flops 15070134272 | bytes 41418752 | tf_op jit(solution)/shard_map/dot_general | solution.py:108
  582.4 24.7 %fusion.1 = (bf16[4096,896]{1,0:T(8,128)(2,1)}, bf16[4096,896]{1,0:T(8,128)(2,1)}) fusion(f32[4096,896]{1,0:T(8,128)} %copy.25, f32[4096,1792]{1,0:T(8,128)} %fusion.5, f32[4096,896]{1,0:T(8,128)} %copy.24), kind=kLoop, calls=%fused_computation.6 | loop fusion | flops 14680064 | bytes 73400320 | tf_op jit(solution)/shard_map/convert_element_type | solution.py:37
  607.0 516.9 %reduce-scatter.5.cloned.1.call-done = f32[64,8192]{1,0:T(8,128)} async-done(((f32[1024,8192]{1,0:T(8,128)}), f32[64,8192]{1,0:T(8,128)}) %reduce-scatter.5.cloned.1.call-update) | async-done | bytes 2097168 | tf_op jit(solution)/shard_map/reduce_scatter | solution.py:94
  1123.9 1.7 convert.4
  1125.6 1.0 fusion.17
  (38 shorter events, 0.2 us)
Async XLA Ops:
  7.2 295.4 %all-gather.3.cloned.1.call-start = ((), (), s32[]{:S(2)}) async-start(), calls=%async_computation.2 | async-start | bytes 8912896 | tf_op jit(solution)/shard_map/all_gather | solution.py:72
  7.9 344.3 %reduce-scatter.3.cloned.1.call-start = ((), (), s32[]{:S(2)}) async-start(), calls=%async_computation.3 | async-start | bytes 16515072 | tf_op jit(solution)/shard_map/reduce_scatter | solution.py:74
  7.9 15.3 %collective-permute-start = (bf16[64,4096]{1,0:T(8,128)(2,1)}, bf16[64,4096]{1,0:T(8,128)(2,1)S(1)}, u32[]{:S(2)}, u32[]{:S(2)}) collective-permute-start(bf16[64,4096]{1,0:T(8,128)(2,1)} %param.11), channel_id=1, source_target_pairs={{0,1},{1,0},{2,3},{3,2},{4,5},{5,4},{6,7},{7,6},{8,9},{9,8},{10,11... | collective-permute-start | bytes 1572872 | tf_op jit(solution)/shard_map/ppermute | solution.py:11
  24.6 79.7 %collective-permute-start.1 = (bf16[128,4096]{1,0:T(8,128)(2,1)S(1)}, bf16[128,4096]{1,0:T(8,128)(2,1)}, u32[]{:S(2)}, u32[]{:S(2)}) collective-permute-start(bf16[128,4096]{1,0:T(8,128)(2,1)S(1)} %maximum_select_fusion.5), channel_id=1, source_target_pairs={{0,2},{1,3},{2,0},{3,1},{4,6},{5,7},{6,4},{7,5},{8,10},{9,11},{10,... | collective-permute-start | bytes 3145736 | tf_op jit(solution)/shard_map/ppermute | solution.py:11
  106.7 77.2 %collective-permute-start.2 = (bf16[256,4096]{1,0:T(8,128)(2,1)S(1)}, bf16[256,4096]{1,0:T(8,128)(2,1)}, u32[]{:S(2)}, u32[]{:S(2)}) collective-permute-start(bf16[256,4096]{1,0:T(8,128)(2,1)S(1)} %maximum_select_fusion.2), channel_id=1, source_target_pairs={{0,4},{1,5},{2,6},{3,7},{4,0},{5,1},{6,2},{7,3},{8,12},{9,13},{10,... | collective-permute-start | bytes 6291464 | tf_op jit(solution)/shard_map/ppermute | solution.py:11
  188.5 91.4 %collective-permute-start.3 = (bf16[512,4096]{1,0:T(8,128)(2,1)}, bf16[512,4096]{1,0:T(8,128)(2,1)}, u32[]{:S(2)}, u32[]{:S(2)}) collective-permute-start(bf16[512,4096]{1,0:T(8,128)(2,1)} %maximum_select_fusion.1), channel_id=1, source_target_pairs={{0,8},{1,9},{2,10},{3,11},{4,12},{5,13},{6,14},{7,15},{8,0},{9,1},... | collective-permute-start | bytes 12582920 | tf_op jit(solution)/shard_map/ppermute | solution.py:11
  200.6 10.9 copy-start.6
  200.6 10.9 copy-start.7
  200.7 11.5 %copy-start.8 = (s32[32,7]{0,1:T(8,128)S(1)}, s32[32,7]{0,1:T(8,128)}, u32[]{:S(2)}) copy-start(s32[32,7]{0,1:T(8,128)} %param.20) | copy-start | bytes 2692
  200.7 11.5 %copy-start.9 = (s32[32,7]{0,1:T(8,128)S(1)}, s32[32,7]{0,1:T(8,128)}, u32[]{:S(2)}) copy-start(s32[32,7]{0,1:T(8,128)} %param.17) | copy-start | bytes 2692
  200.7 12.1 %copy-start.10 = (s32[7,32]{1,0:T(8,128)S(1)}, s32[7,32]{1,0:T(8,128)}, u32[]{:S(2)}) copy-start(s32[7,32]{1,0:T(8,128)} %param.21) | copy-start | bytes 2692
  200.7 12.1 %copy-start.11 = (s32[7,32]{1,0:T(8,128)S(1)}, s32[7,32]{1,0:T(8,128)}, u32[]{:S(2)}) copy-start(s32[7,32]{1,0:T(8,128)} %param.18) | copy-start | bytes 2692
  212.7 6.4 slice-start
  213.4 5.8 slice-start.1
  213.4 7.5 copy-start
  303.6 2.9 copy-start.2
  334.3 40.3 %all-gather.5.cloned.1.call-start = ((), (), s32[]{:S(2)}) async-start(), calls=%async_computation.4 | async-start | bytes 8257536 | tf_op jit(solution)/shard_map/all_gather | solution.py:89
  357.5 766.4 %reduce-scatter.5.cloned.1.call-start = ((), (), s32[]{:S(2)}) async-start(), calls=%async_computation.5 | async-start | bytes 35651584 | tf_op jit(solution)/shard_map/reduce_scatter | solution.py:94
  397.7 16.2 %copy-start.1 = (f32[1024,4096]{1,0:T(8,128)S(1)}, f32[1024,4096]{1,0:T(8,128)}, u32[]{:S(2)}) copy-start(f32[1024,4096]{1,0:T(8,128)} %fusion.3) | copy-start | bytes 50331652
  432.7 0.7 copy-start.5
  466.1 16.2 %copy-start.4 = (f32[32,7]{0,1:T(8,128)S(1)}, f32[32,7]{0,1:T(8,128)}, u32[]{:S(2)}) copy-start(f32[32,7]{0,1:T(8,128)} %get-tuple-element.8) | copy-start | bytes 2692
  514.5 16.2 %copy-start.3 = (f32[7,32]{1,0:T(8,128)S(1)}, f32[7,32]{1,0:T(8,128)}, u32[]{:S(2)}) copy-start(f32[7,32]{1,0:T(8,128)} %get-tuple-element.6) | copy-start | bytes 2692
  530.7 27.8 %slice-start.2 = ((s8[5505024]{0:T(1024)(128)(4,1)}), s8[4194304]{0:T(1024)(128)(4,1)S(1)}, s32[]{:S(2)}) async-start(s8[5505024]{0:T(1024)(128)(4,1)} %bitcast.53), calls=%async_computation.8 | async-start | bytes 8388608
  537.8 20.7 %slice-start.3 = ((s8[5505024]{0:T(1024)(128)(4,1)}), s8[1310720]{0:T(1024)(128)(4,1)S(1)}, s32[]{:S(2)}) async-start(s8[5505024]{0:T(1024)(128)(4,1)} %bitcast.53), calls=%async_computation.9 | async-start | bytes 2621440
Sparse Core Ops, SparseCore 0:
  10.8 180.4 all-gather.2
  334.4 17.6 reduce-scatter.2
  357.7 16.8 all-gather.4
  432.9 691.0 reduce-scatter.4
